TPU v7x, 256 devices: a whole 4x4x8 slice. The times are simulated.
256 devices in a mesh: cuts: 32 (over y_lo, z, core), chan: 8 (over y_hi, x).
Axes of the slice: x: 4, y: 4 (y_hi: 2, y_lo: 2; y = y_hi * 2 + y_lo), z: 8, core: 2. Of those that a mesh axis runs over, the one named last changes fastest.
Arguments:
- data: bfloat16 [256, 384, 1024], P('cuts', None, 'chan'), may hold values from -6 to 6
- order: int32 [256], P('cuts'), may hold values from 0 to 255, as said below
- chan_factor: bfloat16 [1024, 64], P('chan'), may hold values from -0.1875 to 0.1875
- slice_weights: float32 [256, 64], P('cuts'), may hold values from 0.5 to 2
- smooth_aux: float32 [256, 384, 64], P('cuts', 'chan'), may hold values from -6 to 6
- coupled: float32 [256, 384, 64], P('cuts', 'chan'), may hold values from -6 to 6
- smooth_dual: float32 [256, 384, 64], P('cuts', 'chan'), may hold values from -2 to 2
- coupling_dual: float32 [256, 384, 64], P('cuts', 'chan'), may hold values from -2 to 2
- delta: float32 [64, 64], replicated, may hold values from -0.1125 to 1.1125, as said below
Outputs:
- evolving: float32 [256, 384, 64], P('cuts', 'chan')
- coupled_out: float32 [256, 384, 64], P('cuts', 'chan')
- delta_out: float32 [64, 64], replicated
Inputs may be any that keep to these rules, and one draw needn't show every extreme that they name: `order`: within each aligned block of 8 entries (the slices of one index of cuts) the entries are a permutation of that block's own slice indices; entry k names the stored slice of phase bin k. `delta`: A full-rank matrix.
All inputs are finite; a program needn't handle non-finite values.
Results may differ from a plain program's by a relative error of at most 0.0003.
Values sent between devices are 32-bit elements; how exact they have to be, the bound alone decides.
A program may use at most 64 MiB of HBM per device.

v0:
```python
import jax
import jax.numpy as jnp
from jax import lax
from jax.sharding import PartitionSpec as P

INNER = 3
SWEEPS = 4
POLAR = 8
smooth_weight = 1.0
eps_trace = 1e-06
highest = lax.Precision.HIGHEST


def with_halo(cells, sides, width):
    for axis, dim in sides:
        count = lax.axis_size(axis)
        head = lax.slice_in_dim(cells, 0, width, axis=dim)
        tail = lax.slice_in_dim(cells, cells.shape[dim] - width, cells.shape[dim], axis=dim)
        cells = jnp.concatenate(
            [
                lax.ppermute(tail, axis, [(i, (i + 1) % count) for i in range(count)]),
                cells,
                lax.ppermute(head, axis, [((i + 1) % count, i) for i in range(count)]),
            ],
            axis=dim,
        )
    return cells


def setup_system(slice_weights, factor_gram):
    rank = factor_gram.shape[0]
    identity = jnp.eye(rank, dtype=jnp.float32)
    diagonal_gram = jnp.diagonal(factor_gram)
    rho = jnp.sum(slice_weights * slice_weights * diagonal_gram[None, :], axis=1) / rank
    system = slice_weights[:, :, None] * factor_gram[None] * slice_weights[:, None, :]
    system = system + 2.0 * rho[:, None, None] * identity
    factors = jax.vmap(jnp.linalg.cholesky)(system)
    inverse = jax.vmap(lambda lower: jax.scipy.linalg.cho_solve((lower, True), identity))(factors)
    return (rho, inverse)


def polar_terms(gram, delta_now):
    rank = gram.shape[1]
    identity = jnp.eye(rank, dtype=jnp.float32)
    left = jnp.einsum("rs,kst->krt", delta_now, gram, precision=highest)
    normal = jnp.einsum("krt,ut->kru", left, delta_now, precision=highest)
    trace = jnp.trace(normal, axis1=1, axis2=2) + eps_trace
    current = normal / trace[:, None, None]
    root = jnp.broadcast_to(identity, normal.shape)
    for step in range(POLAR):
        bracket = 1.5 * identity - 0.5 * jnp.einsum(
            "krs,kst->krt", root, current, precision=highest
        )
        current = jnp.einsum("krs,kst->krt", current, bracket, precision=highest)
        root = jnp.einsum("krs,kst->krt", bracket, root, precision=highest)
    scale = 1.0 / jnp.sqrt(trace)
    partial_value = jnp.einsum("ksr,st->krt", root, delta_now, precision=highest)
    partial_value = (
        jnp.einsum("krt,ktu->kru", partial_value, gram, precision=highest) * scale[:, None, None]
    )
    return (root, scale, partial_value)


def coupled_update(tall, root, scale, delta_now, delta_new):
    mixer = jnp.einsum("sr,kst->krt", delta_now, root, precision=highest)
    mixer = jnp.einsum("krt,tu->kru", mixer, delta_new, precision=highest) * scale[:, None, None]
    return jnp.einsum("kir,kru->kiu", tall, mixer, precision=highest)


def smooth(aux, target, rho_cols):
    for sweep in range(SWEEPS):
        padded = with_halo(aux, (("cuts", 0),), 1)
        beside = padded[:-2] + padded[2:]
        aux = (rho_cols * target + 2.0 * smooth_weight * beside) / (rho_cols + 4.0 * smooth_weight)
    return aux


def body(
    data, order, chan_factor, slice_weights, smooth_aux, coupled, smooth_dual, coupling_dual, delta
):
    count_slices = data.shape[0]
    total_slices = count_slices * lax.axis_size("cuts")
    summed = lax.psum_scatter(
        jnp.einsum("kij,jr->ikr", data, chan_factor, preferred_element_type=jnp.float32),
        "chan",
        scatter_dimension=0,
        tiled=True,
    )
    local_order = order - lax.axis_index("cuts") * count_slices
    projected = jnp.transpose(jnp.take(summed, local_order, axis=1), (1, 0, 2))
    factor_gram = lax.psum(
        jnp.dot(chan_factor.T, chan_factor, preferred_element_type=jnp.float32), "chan"
    )
    rho, inverse = setup_system(slice_weights, factor_gram)
    data_side = projected * slice_weights[:, None, :]
    rho_cols = rho[:, None, None]
    aux = smooth_aux
    coup = coupled
    dual_s = smooth_dual
    dual_c = coupling_dual
    delta_now = delta
    evolving = aux
    for inner in range(INNER):
        rhs = data_side + rho_cols * (aux - dual_s + coup - dual_c)
        evolving = jnp.einsum("kir,krs->kis", rhs, inverse, precision=highest)
        target = evolving + dual_s
        aux = smooth(aux, target, rho_cols)
        tall = evolving + dual_c
        whole = lax.all_gather(tall, "chan", axis=1, tiled=True)
        gram = jnp.einsum("kir,kis->krs", whole, whole, precision=highest)
        root, scale, partial_value = polar_terms(gram, delta_now)
        delta_new = lax.psum(jnp.sum(partial_value, axis=0), "cuts") / total_slices
        coup = coupled_update(tall, root, scale, delta_now, delta_new)
        dual_s = dual_s + evolving - aux
        dual_c = dual_c + evolving - coup
        delta_now = delta_new
    return (evolving, coup, delta_now)


def solution(mesh):
    return jax.shard_map(
        body,
        mesh=mesh,
        in_specs=(
            P("cuts", None, "chan"),
            P("cuts"),
            P("chan", None),
            P("cuts", None),
            P("cuts", "chan", None),
            P("cuts", "chan", None),
            P("cuts", "chan", None),
            P("cuts", "chan", None),
            P(),
        ),
        out_specs=(P("cuts", "chan", None), P("cuts", "chan", None), P()),
        check_vma=False,
    )
```

profile of v0, /device:TPU:8, one launch (start us, length us, event | category | flops | bytes accessed | tf_op | source)
XLA Modules:
  0.0 663.4 jit_solution(12568983401531240565)
XLA Ops:
  8.0 5.2 collective-permute-start.1
  13.2 1.1 convolution_bitcast_fusion
  14.4 1.6 copy.125
  16.2 41.4 %psum.28 = f32[64,64]{1,0:T(8,128)S(1)} all-reduce(f32[64,64]{1,0:T(8,128)S(1)} %fusion.188), channel_id=1, replica_groups=mesh['cuts'=32,'chan'=8] {'chan'}, use_global_device_ids=true, to_apply=%region_1.2 | all-reduce | flops 4096 | bytes 32768 | tf_op jit(solution)/shard_map/psum | solution.py:91
  58.9 46.9 %custom-call.11 = f32[8,64,64]{2,1,0:T(8,128)S(1)} custom-call(f32[8,64,64]{2,1,0:T(8,128)S(1)} %add_multiply_fusion), custom_call_target="Cholesky" | custom-call | tf_op jit(solution)/shard_map/vmap(jit(cholesky))/cholesky | solution.py:37
  106.0 39.3 %custom-call.12 = f32[8,1,64,64]{2,3,1,0:T(8,128)S(1)} custom-call(f32[8,1,64,64]{3,2,1,0:T(8,128)S(1)} %select_bitcast_fusion), custom_call_target="InvertDiagBlocksLowerTriangular" | custom-call | tf_op jit(solution)/shard_map/vmap(jit(_cho_solve))/triangular_solve | solution.py:38
  146.5 1.0 copy.126
  148.6 36.8 %all_gather.9 = f32[8,384,64]{2,0,1:T(8,128)S(1)} all-gather(f32[8,48,64]{2,0,1:T(8,128)S(1)} %copy.129), channel_id=1, replica_groups=mesh['cuts'=32,'chan'=8] {'chan'}, dimensions={1}, use_global_device_ids=true | all-gather | bytes 884736 | tf_op jit(solution)/shard_map/all_gather | solution.py:109
  185.5 3.0 fusion.4
  201.0 3.2 collective-permute-done.2
  204.8 108.0 %psum.29 = f32[64,64]{1,0:T(8,128)S(1)} all-reduce(f32[64,64]{1,0:T(8,128)S(1)} %fusion.30), channel_id=1, replica_groups=mesh['cuts'=32,'chan'=8] {'cuts'}, use_global_device_ids=true, to_apply=%region_7.8 | all-reduce | flops 4096 | bytes 32768 | tf_op jit(solution)/shard_map/psum | solution.py:112
  314.6 3.9 collective-permute-done.6
  320.3 3.9 collective-permute-done.8
  324.8 37.0 %all_gather.10 = f32[8,384,64]{2,0,1:T(8,128)S(1)} all-gather(f32[8,48,64]{2,0,1:T(8,128)S(1)} %copy.136), channel_id=1, replica_groups=mesh['cuts'=32,'chan'=8] {'chan'}, dimensions={1}, use_global_device_ids=true | all-gather | bytes 884736 | tf_op jit(solution)/shard_map/all_gather | solution.py:109
  361.8 3.0 fusion.2
  377.1 107.8 %psum.30 = f32[64,64]{1,0:T(8,128)S(1)} all-reduce(f32[64,64]{1,0:T(8,128)S(1)} %fusion.31), channel_id=1, replica_groups=mesh['cuts'=32,'chan'=8] {'cuts'}, use_global_device_ids=true, to_apply=%region_10.11 | all-reduce | flops 4096 | bytes 32768 | tf_op jit(solution)/shard_map/psum | solution.py:112
  486.7 3.9 collective-permute-done.12
  492.3 3.9 collective-permute-done.14
  496.3 1.2 fusion.187
  497.6 37.6 %all_gather.11 = f32[8,384,64]{2,0,1:T(8,128)S(1)} all-gather(f32[8,48,64]{2,0,1:T(8,128)S(1)} %copy.143), channel_id=1, replica_groups=mesh['cuts'=32,'chan'=8] {'chan'}, dimensions={1}, use_global_device_ids=true | all-gather | bytes 884736 | tf_op jit(solution)/shard_map/all_gather | solution.py:109
  535.2 3.0 fusion
  548.3 0.9 fusion.227
  550.0 104.4 %psum.31 = f32[64,64]{1,0:T(8,128)S(1)} all-reduce(f32[64,64]{1,0:T(8,128)S(1)} %fusion.32), channel_id=1, replica_groups=mesh['cuts'=32,'chan'=8] {'cuts'}, use_global_device_ids=true, to_apply=%region_13.14 | all-reduce | flops 4096 | bytes 32768 | tf_op jit(solution)/shard_map/psum | solution.py:112
  655.0 1.1 fusion.228
  (175 shorter events, 48.5 us)
Async XLA Ops:
  7.2 139.3 %reduce-scatter.2.cloned.1.call-start = ((), (), s32[]{:S(2)}) async-start(), calls=%async_computation.1 | async-start | bytes 1769472 | tf_op jit(solution)/shard_map/reduce_scatter | solution.py:83
  8.0 140.0 %collective-permute-start.1 = (f32[1,48,64]{2,1,0:T(8,128)S(1)}, f32[1,48,64]{2,1,0:T(8,128)S(1)}, u32[]{:S(2)}, u32[]{:S(2)}) collective-permute-start(f32[1,48,64]{2,1,0:T(8,128)S(1)} %get-tuple-element.28), channel_id=1, source_target_pairs={{8,0},{16,8},{24,16},{32,24},{40,32},{48,40},{56,48},{64,56},{72,6... | collective-permute-start | bytes 36872 | tf_op jit(solution)/shard_map/ppermute | solution.py:23
  13.2 134.8 %collective-permute-start = (f32[1,48,64]{2,1,0:T(8,128)S(1)}, f32[1,48,64]{2,1,0:T(8,128)S(1)}, u32[]{:S(2)}, u32[]{:S(2)}) collective-permute-start(f32[1,48,64]{2,1,0:T(8,128)S(1)} %get-tuple-element.27), channel_id=1, source_target_pairs={{0,8},{8,16},{16,24},{24,32},{32,40},{40,48},{48,56},{56,64},{64,7... | collective-permute-start | bytes 36872 | tf_op jit(solution)/shard_map/ppermute | solution.py:21
  16.0 42.4 %copy-start.6 = (f32[8,64]{1,0:T(8,128)S(1)}, f32[8,64]{1,0:T(8,128)}, u32[]{:S(2)}) copy-start(f32[8,64]{1,0:T(8,128)} %param.12) | copy-start | bytes 6148
  16.0 129.4 %copy-start.9 = (s32[8]{0:T(128)S(1)}, s32[8]{0:T(128)}, u32[]{:S(2)}) copy-start(s32[8]{0:T(128)} %param.10) | copy-start | bytes 100
  58.8 89.2 %copy-start.1 = (f32[8,48,64]{2,1,0:T(8,128)S(1)}, f32[8,48,64]{2,1,0:T(8,128)}, u32[]{:S(2)}) copy-start(f32[8,48,64]{2,1,0:T(8,128)} %param.13) | copy-start | bytes 294916
  58.8 89.2 %copy-start.3 = (f32[8,48,64]{2,1,0:T(8,128)S(1)}, f32[8,48,64]{2,1,0:T(8,128)}, u32[]{:S(2)}) copy-start(f32[8,48,64]{2,1,0:T(8,128)} %param.15) | copy-start | bytes 294916
  58.8 89.2 %copy-start.4 = (f32[8,48,64]{2,1,0:T(8,128)S(1)}, f32[8,48,64]{2,1,0:T(8,128)}, u32[]{:S(2)}) copy-start(f32[8,48,64]{2,1,0:T(8,128)} %param.16) | copy-start | bytes 294916
  58.8 89.2 %copy-start.5 = (f32[8,48,64]{2,1,0:T(8,128)S(1)}, f32[8,48,64]{2,1,0:T(8,128)}, u32[]{:S(2)}) copy-start(f32[8,48,64]{2,1,0:T(8,128)} %param.14) | copy-start | bytes 294916
  148.6 39.8 %copy-start.2 = (f32[64,64]{1,0:T(8,128)S(1)}, f32[64,64]{1,0:T(8,128)}, u32[]{:S(2)}) copy-start(f32[64,64]{1,0:T(8,128)} %param.17) | copy-start | bytes 49156
  198.2 2.8 collective-permute-start.3
  198.7 5.4 collective-permute-start.2
  204.3 108.6 %collective-permute-start.5 = (f32[1,48,64]{2,1,0:T(8,128)S(1)}, f32[1,48,64]{2,1,0:T(8,128)S(1)}, u32[]{:S(2)}, u32[]{:S(2)}) collective-permute-start(f32[1,48,64]{2,1,0:T(8,128)S(1)} %get-tuple-element.23), channel_id=1, source_target_pairs={{8,0},{16,8},{24,16},{32,24},{40,32},{48,40},{56,48},{64,56},{72,6... | collective-permute-start | bytes 36872 | tf_op jit(solution)/shard_map/ppermute | solution.py:23
  204.6 108.3 %collective-permute-start.4 = (f32[1,48,64]{2,1,0:T(8,128)S(1)}, f32[1,48,64]{2,1,0:T(8,128)S(1)}, u32[]{:S(2)}, u32[]{:S(2)}) collective-permute-start(f32[1,48,64]{2,1,0:T(8,128)S(1)} %get-tuple-element.22), channel_id=1, source_target_pairs={{0,8},{8,16},{16,24},{24,32},{32,40},{40,48},{48,56},{56,64},{64,7... | collective-permute-start | bytes 36872 | tf_op jit(solution)/shard_map/ppermute | solution.py:21
  313.0 1.6 collective-permute-start.7
  313.1 5.4 collective-permute-start.6
  318.7 1.6 collective-permute-start.9
  318.8 5.4 collective-permute-start.8
  376.1 108.8 %collective-permute-start.11 = (f32[1,48,64]{2,1,0:T(8,128)S(1)}, f32[1,48,64]{2,1,0:T(8,128)S(1)}, u32[]{:S(2)}, u32[]{:S(2)}) collective-permute-start(f32[1,48,64]{2,1,0:T(8,128)S(1)} %get-tuple-element.16), channel_id=1, source_target_pairs={{8,0},{16,8},{24,16},{32,24},{40,32},{48,40},{56,48},{64,56},{72,6... | collective-permute-start | bytes 36872 | tf_op jit(solution)/shard_map/ppermute | solution.py:23
  376.2 108.8 %collective-permute-start.10 = (f32[1,48,64]{2,1,0:T(8,128)S(1)}, f32[1,48,64]{2,1,0:T(8,128)S(1)}, u32[]{:S(2)}, u32[]{:S(2)}) collective-permute-start(f32[1,48,64]{2,1,0:T(8,128)S(1)} %get-tuple-element.15), channel_id=1, source_target_pairs={{0,8},{8,16},{16,24},{24,32},{32,40},{40,48},{48,56},{56,64},{64,7... | collective-permute-start | bytes 36872 | tf_op jit(solution)/shard_map/ppermute | solution.py:21
  485.1 1.6 collective-permute-start.13
  485.2 5.4 collective-permute-start.12
  490.7 1.6 collective-permute-start.15
  490.8 5.4 collective-permute-start.14
  (3 other events, 9.4 us)
Sparse Core Ops, SparseCore 0:
  16.1 78.8 reduce-scatter.1
where the time goes:
time: 669 us; the launch traced here: 663 us
  blocking collectives  473 us (71%)
  other arithmetic  87.4 us (13%)
  matrix products  51.3 us (8%)
  waiting for transfers between devices  21 us (3%)
  between operations  15.6 us (2%)
  starting transfers between devices  9.69 us (1%)
    psum x3, blocking collectives, body(): delta_new = lax.psum(jnp.sum(partial_value, axis=0), 'cuts') / total_slices  320 us
    all_gather x3, blocking collectives, body(): whole = lax.all_gather(tall, 'chan', axis=1, tiled=True)  111 us
    another operation x4, other arithmetic, setup_system(): factors = jax.vmap(jnp.linalg.cholesky)(system)  47.1 us
    psum x1, blocking collectives, body(): lax.psum(jnp.dot(chan_factor.T, chan_factor, preferred_element_type=jnp.f...  41.4 us
    another operation x3, other arithmetic, setup_system(): jax.scipy.linalg.cho_solve((lower, True), identity)  39.4 us
    ppermute x8, waiting for transfers between devices, with_halo(): lax.ppermute(tail, axis, [(i, (i + 1) % count) for i in range(count)])  18.9 us
  transfers between devices with their start and end apart: 17, of which 9 were waited for; matrix products, arithmetic and copies ran while one was open for 15% of the time, Pallas kernels for 0%

commit v1 on v0

--- a/solution.py
+++ b/solution.py
@@ -106,7 +106,9 @@
         target = evolving + dual_s
         aux = smooth(aux, target, rho_cols)
         tall = evolving + dual_c
-        whole = lax.all_gather(tall, "chan", axis=1, tiled=True)
+        whole = jnp.concatenate(
+            lax.all_to_all(jnp.stack([tall] * lax.axis_size("chan")), "chan", 0, 0), axis=1
+        )
         gram = jnp.einsum("kir,kis->krs", whole, whole, precision=highest)
         root, scale, partial_value = polar_terms(gram, delta_now)
         delta_new = lax.psum(jnp.sum(partial_value, axis=0), "cuts") / total_slices

time: 669 us -> 623 us (0.931)
  blocking collectives: 473 us -> 374 us
  local copies, waits for them, and re-layouts: 5.17 us -> 28.5 us
  starting transfers between devices: 9.69 us -> 26 us
  other arithmetic: 87.4 us -> 95.5 us
    all_gather x3 -> x0, blocking collectives: 111 us -> none  [body(): whole = lax.all_gather(tall, 'chan', axis=1, tiled=True)]
    all_to_all x0 -> x1, blocking collectives: none -> 16.4 us  [body(): lax.all_to_all(jnp.stack([tall] * lax.axis_size('chan')), 'chan', 0, 0)]
    unnamed x20 -> x60, local copies, waits for them, and re-layouts: 0.06 us -> 11.1 us
    reshape x0 -> x6, local copies, waits for them, and re-layouts: none -> 10.9 us  [body(): jnp.concatenate(lax.all_to_all(jnp.stack([tall] * lax.axis_size('chan')),...]
    all_to_all x0 -> x2, starting transfers between devices: none -> 10.2 us  [body(): lax.all_to_all(jnp.stack([tall] * lax.axis_size('chan')), 'chan', 0, 0)]
    all_to_all x0 -> x3, other arithmetic: none -> 7.46 us  [body(): lax.all_to_all(jnp.stack([tall] * lax.axis_size('chan')), 'chan', 0, 0)]
    all_to_all x0 -> x2, waiting for transfers between devices: none -> 7.13 us  [body(): lax.all_to_all(jnp.stack([tall] * lax.axis_size('chan')), 'chan', 0, 0)]
  transfers between devices with their start and end apart: 17 -> 19, of which waited for: 9 -> 8; matrix products, arithmetic and copies ran while one was open for 15% -> 24% of each run, Pallas kernels for 0% -> 0%
where the time goes in v1:
time: 623 us; the launch traced here: 613 us
  blocking collectives  374 us (60%)
  other arithmetic  95.5 us (15%)
  matrix products  49.6 us (8%)
  local copies, waits for them, and re-layouts  28.5 us (5%)
  starting transfers between devices  26 us (4%)
  waiting for transfers between devices  23.5 us (4%)
  between operations  15.8 us (3%)
    psum x3, blocking collectives, body(): delta_new = lax.psum(jnp.sum(partial_value, axis=0), 'cuts') / total_slices  317 us
    another operation x4, other arithmetic, setup_system(): factors = jax.vmap(jnp.linalg.cholesky)(system)  47.1 us
    psum x1, blocking collectives, body(): lax.psum(jnp.dot(chan_factor.T, chan_factor, preferred_element_type=jnp.f...  41.4 us
    another operation x3, other arithmetic, setup_system(): jax.scipy.linalg.cho_solve((lower, True), identity)  39.4 us
    all_to_all x1, blocking collectives, body(): lax.all_to_all(jnp.stack([tall] * lax.axis_size('chan')), 'chan', 0, 0)  16.4 us
    ppermute x8, starting transfers between devices, with_halo(): lax.ppermute(head, axis, [((i + 1) % count, i) for i in range(count)])  12.8 us
    ppermute x8, waiting for transfers between devices, with_halo(): lax.ppermute(tail, axis, [(i, (i + 1) % count) for i in range(count)])  12.7 us
  transfers between devices with their start and end apart: 19, of which 8 were waited for; matrix products, arithmetic and copies ran while one was open for 24% of the time, Pallas kernels for 0%

profile of v1, /device:TPU:8, one launch (start us, length us, event | category | flops | bytes accessed | tf_op | source)
XLA Modules:
  0.0 613.3 jit_solution(3343361535305420372)
XLA Ops:
  8.0 5.2 collective-permute-start.1
  16.2 41.4 %psum.28 = f32[64,64]{1,0:T(8,128)S(1)} all-reduce(f32[64,64]{1,0:T(8,128)S(1)} %fusion.182), channel_id=1, replica_groups=mesh['cuts'=32,'chan'=8] {'chan'}, use_global_device_ids=true, to_apply=%region_1.2 | all-reduce | flops 4096 | bytes 32768 | tf_op jit(solution)/shard_map/psum | solution.py:91
  58.9 46.9 %custom-call.11 = f32[8,64,64]{2,1,0:T(8,128)S(1)} custom-call(f32[8,64,64]{2,1,0:T(8,128)S(1)} %add_multiply_fusion), custom_call_target="Cholesky" | custom-call | tf_op jit(solution)/shard_map/vmap(jit(cholesky))/cholesky | solution.py:37
  106.1 39.3 %custom-call.12 = f32[8,1,64,64]{2,3,1,0:T(8,128)S(1)} custom-call(f32[8,1,64,64]{3,2,1,0:T(8,128)S(1)} %select_bitcast_fusion), custom_call_target="InvertDiagBlocksLowerTriangular" | custom-call | tf_op jit(solution)/shard_map/vmap(jit(_cho_solve))/triangular_solve | solution.py:38
  150.2 3.9 collective-permute-done.2
  156.9 3.7 all-to-all-start
  160.7 3.5 collective-permute-start.7
  165.7 4.7 collective-permute-done.6
  172.3 3.0 all-to-all-done
  175.8 2.5 reduce.6
  183.7 2.4 fusion.183
  197.7 105.2 %psum.29 = f32[64,64]{1,0:T(8,128)S(1)} all-reduce(f32[64,64]{1,0:T(8,128)S(1)} %fusion.24), channel_id=1, replica_groups=mesh['cuts'=32,'chan'=8] {'cuts'}, use_global_device_ids=true, to_apply=%region_7.8 | all-reduce | flops 4096 | bytes 32768 | tf_op jit(solution)/shard_map/psum | solution.py:114
  307.1 6.5 %all-to-all-start.1 = ((f32[8,1,24576]{2,1,0:T(1,128)}), f32[8,1,24576]{2,1,0:T(1,128)S(1)}, u32[]{:S(2)}, u32[]{:S(2)}) async-start(f32[8,1,24576]{2,1,0:T(1,128)} %reshape.123), calls=%async_computation.2 | async-start | bytes 1572864 | tf_op jit(solution)/shard_map/all_to_all | solution.py:110
  313.7 3.8 collective-permute-start.13
  319.1 4.1 collective-permute-done.12
  323.9 4.2 all-to-all-done.1
  328.1 2.5 reduce.7
  336.0 2.4 fusion.197
  349.9 105.1 %psum.30 = f32[64,64]{1,0:T(8,128)S(1)} all-reduce(f32[64,64]{1,0:T(8,128)S(1)} %fusion.25), channel_id=1, replica_groups=mesh['cuts'=32,'chan'=8] {'cuts'}, use_global_device_ids=true, to_apply=%region_10.11 | all-reduce | flops 4096 | bytes 32768 | tf_op jit(solution)/shard_map/psum | solution.py:114
  459.8 16.4 %all_to_all.15 = f32[8,1,24576]{2,1,0:T(1,128)S(1)} all-to-all(f32[8,1,24576]{2,1,0:T(1,128)S(1)} %reshape.125), channel_id=1, replica_groups=mesh['cuts'=32,'chan'=8] {'chan'}, dimensions={0} | all-to-all | bytes 1572864 | tf_op jit(solution)/shard_map/all_to_all | solution.py:110
  476.2 2.5 reduce.8
  480.5 2.2 copy.115
  484.2 2.4 fusion.211
  498.0 106.3 %psum.31 = f32[64,64]{1,0:T(8,128)S(1)} all-reduce(f32[64,64]{1,0:T(8,128)S(1)} %fusion.26), channel_id=1, replica_groups=mesh['cuts'=32,'chan'=8] {'cuts'}, use_global_device_ids=true, to_apply=%region_13.14 | all-reduce | flops 4096 | bytes 32768 | tf_op jit(solution)/shard_map/psum | solution.py:114
  (227 shorter events, 77.5 us)
Async XLA Ops:
  7.2 139.3 %reduce-scatter.2.cloned.1.call-start = ((), (), s32[]{:S(2)}) async-start(), calls=%async_computation.4 | async-start | bytes 1769472 | tf_op jit(solution)/shard_map/reduce_scatter | solution.py:83
  8.0 139.9 %collective-permute-start.1 = (f32[1,48,64]{2,1,0:T(8,128)S(1)}, f32[1,48,64]{2,1,0:T(8,128)S(1)}, u32[]{:S(2)}, u32[]{:S(2)}) collective-permute-start(f32[1,48,64]{2,1,0:T(8,128)S(1)} %get-tuple-element.28), channel_id=1, source_target_pairs={{8,0},{16,8},{24,16},{32,24},{40,32},{48,40},{56,48},{64,56},{72,6... | collective-permute-start | bytes 36872 | tf_op jit(solution)/shard_map/ppermute | solution.py:23
  13.2 134.8 %collective-permute-start = (f32[1,48,64]{2,1,0:T(8,128)S(1)}, f32[1,48,64]{2,1,0:T(8,128)S(1)}, u32[]{:S(2)}, u32[]{:S(2)}) collective-permute-start(f32[1,48,64]{2,1,0:T(8,128)S(1)} %get-tuple-element.27), channel_id=1, source_target_pairs={{0,8},{8,16},{16,24},{24,32},{32,40},{40,48},{48,56},{56,64},{64,7... | collective-permute-start | bytes 36872 | tf_op jit(solution)/shard_map/ppermute | solution.py:21
  16.0 129.4 %copy-start.26 = (s32[8]{0:T(128)S(1)}, s32[8]{0:T(128)}, u32[]{:S(2)}) copy-start(s32[8]{0:T(128)} %param.10) | copy-start | bytes 100
  148.6 1.6 collective-permute-start.3
  148.6 5.4 collective-permute-start.2
  154.2 6.3 %collective-permute-start.5 = (f32[1,48,64]{2,1,0:T(8,128)S(1)}, f32[1,48,64]{2,1,0:T(8,128)S(1)}, u32[]{:S(2)}, u32[]{:S(2)}) collective-permute-start(f32[1,48,64]{2,1,0:T(8,128)S(1)} %get-tuple-element.23), channel_id=1, source_target_pairs={{8,0},{16,8},{24,16},{32,24},{40,32},{48,40},{56,48},{64,56},{72,6... | collective-permute-start | bytes 36872 | tf_op jit(solution)/shard_map/ppermute | solution.py:23
  154.3 6.3 %collective-permute-start.4 = (f32[1,48,64]{2,1,0:T(8,128)S(1)}, f32[1,48,64]{2,1,0:T(8,128)S(1)}, u32[]{:S(2)}, u32[]{:S(2)}) collective-permute-start(f32[1,48,64]{2,1,0:T(8,128)S(1)} %get-tuple-element.22), channel_id=1, source_target_pairs={{0,8},{8,16},{16,24},{24,32},{32,40},{40,48},{48,56},{56,64},{64,7... | collective-permute-start | bytes 36872 | tf_op jit(solution)/shard_map/ppermute | solution.py:21
  156.9 18.4 %all-to-all-start = ((f32[8,1,24576]{2,1,0:T(1,128)}), f32[8,1,24576]{2,1,0:T(1,128)S(1)}, u32[]{:S(2)}, u32[]{:S(2)}) async-start(f32[8,1,24576]{2,1,0:T(1,128)} %reshape.121), calls=%async_computation.1 | async-start | bytes 1572864 | tf_op jit(solution)/shard_map/all_to_all | solution.py:110
  160.7 5.0 collective-permute-start.7
  164.2 6.2 %collective-permute-start.6 = (f32[1,48,64]{2,1,0:T(8,128)S(1)}, f32[1,48,64]{2,1,0:T(8,128)S(1)}, u32[]{:S(2)}, u32[]{:S(2)}) collective-permute-start(f32[1,48,64]{2,1,0:T(8,128)S(1)} %get-tuple-element.20), channel_id=1, source_target_pairs={{0,8},{8,16},{16,24},{24,32},{32,40},{40,48},{48,56},{56,64},{64,7... | collective-permute-start | bytes 36872 | tf_op jit(solution)/shard_map/ppermute | solution.py:21
  171.8 132.1 %collective-permute-start.9 = (f32[1,48,64]{2,1,0:T(8,128)}, f32[1,48,64]{2,1,0:T(8,128)S(1)}, u32[]{:S(2)}, u32[]{:S(2)}) collective-permute-start(f32[1,48,64]{2,1,0:T(8,128)} %get-tuple-element.19), channel_id=1, source_target_pairs={{8,0},{16,8},{24,16},{32,24},{40,32},{48,40},{56,48},{64,56},{72,6... | collective-permute-start | bytes 36872 | tf_op jit(solution)/shard_map/ppermute | solution.py:23
  171.8 132.1 %collective-permute-start.8 = (f32[1,48,64]{2,1,0:T(8,128)S(1)}, f32[1,48,64]{2,1,0:T(8,128)S(1)}, u32[]{:S(2)}, u32[]{:S(2)}) collective-permute-start(f32[1,48,64]{2,1,0:T(8,128)S(1)} %get-tuple-element.18), channel_id=1, source_target_pairs={{0,8},{8,16},{16,24},{24,32},{32,40},{40,48},{48,56},{56,64},{64,7... | collective-permute-start | bytes 36872 | tf_op jit(solution)/shard_map/ppermute | solution.py:21
  195.9 107.6 %copy-start.6 = (f32[8,48,64]{2,1,0:T(8,128)S(1)}, f32[8,48,64]{2,1,0:T(8,128)}, u32[]{:S(2)}) copy-start(f32[8,48,64]{2,1,0:T(8,128)} %copy-done.5) | copy-start | bytes 294916
  196.3 107.6 %copy-start.14 = (f32[8,48,64]{2,1,0:T(8,128)S(1)}, f32[8,48,64]{2,1,0:T(8,128)}, u32[]{:S(2)}) copy-start(f32[8,48,64]{2,1,0:T(8,128)} %copy-done.13) | copy-start | bytes 294916
  196.3 107.6 %copy-start.17 = (f32[8,48,64]{2,1,0:T(8,128)S(1)}, f32[8,48,64]{2,1,0:T(8,128)}, u32[]{:S(2)}) copy-start(f32[8,48,64]{2,1,0:T(8,128)} %get-tuple-element.5) | copy-start | bytes 294916
  304.4 9.2 %collective-permute-start.11 = (f32[1,48,64]{2,1,0:T(8,128)S(1)}, f32[1,48,64]{2,1,0:T(8,128)S(1)}, u32[]{:S(2)}, u32[]{:S(2)}) collective-permute-start(f32[1,48,64]{2,1,0:T(8,128)S(1)} %get-tuple-element.16), channel_id=1, source_target_pairs={{8,0},{16,8},{24,16},{32,24},{40,32},{48,40},{56,48},{64,56},{72,6... | collective-permute-start | bytes 36872 | tf_op jit(solution)/shard_map/ppermute | solution.py:23
  304.5 9.1 %collective-permute-start.10 = (f32[1,48,64]{2,1,0:T(8,128)S(1)}, f32[1,48,64]{2,1,0:T(8,128)S(1)}, u32[]{:S(2)}, u32[]{:S(2)}) collective-permute-start(f32[1,48,64]{2,1,0:T(8,128)S(1)} %get-tuple-element.15), channel_id=1, source_target_pairs={{0,8},{8,16},{16,24},{24,32},{32,40},{40,48},{48,56},{56,64},{64,7... | collective-permute-start | bytes 36872 | tf_op jit(solution)/shard_map/ppermute | solution.py:21
  307.1 21.1 %all-to-all-start.1 = ((f32[8,1,24576]{2,1,0:T(1,128)}), f32[8,1,24576]{2,1,0:T(1,128)S(1)}, u32[]{:S(2)}, u32[]{:S(2)}) async-start(f32[8,1,24576]{2,1,0:T(1,128)} %reshape.123), calls=%async_computation.2 | async-start | bytes 1572864 | tf_op jit(solution)/shard_map/all_to_all | solution.py:110
  313.7 5.3 collective-permute-start.13
  317.5 5.6 collective-permute-start.12
  323.3 132.7 %collective-permute-start.15 = (f32[1,48,64]{2,1,0:T(8,128)S(1)}, f32[1,48,64]{2,1,0:T(8,128)S(1)}, u32[]{:S(2)}, u32[]{:S(2)}) collective-permute-start(f32[1,48,64]{2,1,0:T(8,128)S(1)} %get-tuple-element.12), channel_id=1, source_target_pairs={{8,0},{16,8},{24,16},{32,24},{40,32},{48,40},{56,48},{64,56},{72,6... | collective-permute-start | bytes 36872 | tf_op jit(solution)/shard_map/ppermute | solution.py:23
  323.4 132.7 %collective-permute-start.14 = (f32[1,48,64]{2,1,0:T(8,128)S(1)}, f32[1,48,64]{2,1,0:T(8,128)}, u32[]{:S(2)}, u32[]{:S(2)}) collective-permute-start(f32[1,48,64]{2,1,0:T(8,128)S(1)} %get-tuple-element.11), channel_id=1, source_target_pairs={{0,8},{8,16},{16,24},{24,32},{32,40},{40,48},{48,56},{56,64},{64,7... | collective-permute-start | bytes 36872 | tf_op jit(solution)/shard_map/ppermute | solution.py:21
  496.3 108.7 %copy-start.4 = (f32[8,48,64]{2,1,0:T(8,128)S(1)}, f32[8,48,64]{2,1,0:T(8,128)}, u32[]{:S(2)}) copy-start(f32[8,48,64]{2,1,0:T(8,128)} %copy-done.3) | copy-start | bytes 294916
  (22 other events, 780.5 us)
Sparse Core Ops, SparseCore 0:
  16.2 79.0 reduce-scatter.1
